TPU v7x, 32 devices: a whole 2x2x4 slice. The times are simulated.
32 devices in a mesh: blk: 4 (over x, core), inner: 8 (over z, y).
Axes of the slice: x: 2, y: 2, z: 4, core: 2. Of those that a mesh axis runs over, the one named last changes fastest.
Arguments:
- queries: bfloat16 [4096, 1024], P(('blk', 'inner')), may hold values from -9 to 9
- keys: bfloat16 [4096, 128], P(('blk', 'inner')), may hold values from -4 to 4
- values: bfloat16 [4096, 128], P(('blk', 'inner')), may hold values from -6 to 6
- out_grad: bfloat16 [4096, 1024], P(('blk', 'inner')), may hold values from -6 to 6
- block_list: int32 [32, 5], P(('blk', 'inner')), may hold values from 0 to 31, as said below
Outputs:
- attended: bfloat16 [4096, 1024], P(('blk', 'inner'))
- grad_queries: bfloat16 [4096, 1024], P(('blk', 'inner'))
- grad_keys: float32 [4096, 128], P(('blk', 'inner'))
- grad_values: float32 [4096, 128], P(('blk', 'inner'))
Inputs may be any that keep to these rules, and one draw needn't show every extreme that they name: `block_list`: for query block q, entry n < 2 is max(q - min(n, w - 1), 0) with one w of 2 to 2 a row; each entry n >= 2 is a * 8 for some a with a * 8 <= q.
All inputs are finite; a program needn't handle non-finite values.
Results may differ from a plain program's by a relative error of at most 0.0095.
Values may be sent and summed in bfloat16 or wider, within the bound.
A program may use at most 64 MiB of HBM per device.

v0:
```python
import jax
import jax.numpy as jnp
from jax import lax
from jax.sharding import PartitionSpec as P

HEADS = 8
HEAD_DIM = 128
BLOCK = 128
STRIPES = 3
BAND = 2
NEG = -1e30


def from_behind(block, axis, distance):
    devices = range(lax.axis_size(axis))
    route = [(i - distance, i) for i in devices if i - distance in devices]
    return lax.ppermute(block, axis, route)


def broadcast(value, axis, root):
    mine = lax.axis_index(axis) == root
    return lax.psum(jnp.where(mine, value, jnp.zeros_like(value)), axis)


def shards(queries, keys, values, out_grad, block_list):
    tok_count = keys.shape[0]
    blocks_dev = tok_count // BLOCK
    band_len = BAND
    stripes = STRIPES
    entries = band_len + stripes
    scale = HEAD_DIM ** (-0.5)
    device = lax.axis_index(("blk", "inner"))
    group_blocks = lax.axis_size("inner") * blocks_dev
    groups = lax.axis_size("blk")
    own_blocks = device * blocks_dev + jnp.arange(blocks_dev, dtype=jnp.int32)
    pair = jnp.stack([keys, values])
    earlier = from_behind(pair, ("blk", "inner"), 1)
    window = jnp.concatenate([earlier, pair], axis=1)
    band_pairs = jnp.stack([window])
    column = lax.all_gather(pair[None], "blk", axis=0, tiled=True)
    anchors = broadcast(column, "inner", 0)
    stripe_ids = block_list[:, band_len:]
    anchor_ids = stripe_ids // group_blocks
    picked = anchors[anchor_ids]
    stripe_pairs = jnp.transpose(picked, (0, 2, 1, 3, 4)).reshape(
        blocks_dev, 2, stripes * BLOCK, HEAD_DIM
    )
    key_pairs = jnp.concatenate([band_pairs, stripe_pairs], axis=2)
    band_ids = own_blocks[:, None] - band_len + 1 + jnp.arange(band_len, dtype=jnp.int32)[None, :]
    band_live = (band_ids >= 0) & jnp.any(block_list[:, None, :] == band_ids[:, :, None], axis=2)
    order = jnp.arange(stripes, dtype=jnp.int32)
    before_mask = order[None, :] < order[:, None]
    repeated = jnp.any(
        (stripe_ids[:, :, None] == stripe_ids[:, None, :]) & before_mask[None], axis=2
    )
    in_band = jnp.any(
        (stripe_ids[:, :, None] == band_ids[:, None, :]) & band_live[:, None, :], axis=2
    )
    stripe_live = jnp.logical_not(in_band) & jnp.logical_not(repeated)
    block_live = jnp.concatenate([band_live, stripe_live], axis=1)
    entry_ids = jnp.concatenate([jnp.maximum(band_ids, 0), stripe_ids], axis=1)
    key_tokens = (entry_ids[:, :, None] * BLOCK + jnp.arange(BLOCK, dtype=jnp.int32)).reshape(
        blocks_dev, entries * BLOCK
    )
    live_keys = jnp.repeat(block_live, BLOCK, axis=1)
    query_tokens = own_blocks[:, None] * BLOCK + jnp.arange(BLOCK, dtype=jnp.int32)[None, :]
    allowed = live_keys[:, None, :] & (key_tokens[:, None, :] <= query_tokens[:, :, None])
    heads_per_query = queries.reshape(blocks_dev, BLOCK, HEADS, HEAD_DIM)
    head_gradients = out_grad.reshape(blocks_dev, BLOCK, HEADS, HEAD_DIM)
    key_matrix_rows = key_pairs[:, 0]
    value_matrix_rows = key_pairs[:, 1]
    scores = (
        jnp.einsum(
            "rgao,rmo->ragm", heads_per_query, key_matrix_rows, preferred_element_type=jnp.float32
        )
        * scale
    )
    scores = jnp.where(allowed[:, None], scores, NEG)
    peak = jnp.max(scores, axis=-1, keepdims=True)
    weights = jnp.exp(scores - peak)
    probs = weights / jnp.sum(weights, axis=-1, keepdims=True)
    reduced_probabilities = probs.astype(jnp.bfloat16)
    attended = jnp.einsum(
        "xjaz,xzl->xajl",
        reduced_probabilities,
        value_matrix_rows,
        preferred_element_type=jnp.float32,
    ).astype(jnp.bfloat16)
    grad_probs = jnp.einsum(
        "rgao,rmo->ragm", head_gradients, value_matrix_rows, preferred_element_type=jnp.float32
    )
    delta = jnp.einsum(
        "bihd,bihd->bhi", head_gradients, attended, preferred_element_type=jnp.float32
    )
    score_gradients = (probs * (grad_probs - delta[:, :, :, None]) * scale).astype(jnp.bfloat16)
    grad_queries = jnp.einsum(
        "xjaz,xzl->xajl", score_gradients, key_matrix_rows, preferred_element_type=jnp.float32
    ).astype(jnp.bfloat16)
    grad_key_rows = jnp.einsum(
        "wutc,wtun->wcn", score_gradients, heads_per_query, preferred_element_type=jnp.float32
    )
    grad_value_rows = jnp.einsum(
        "wutc,wtun->wcn", reduced_probabilities, head_gradients, preferred_element_type=jnp.float32
    )
    grad_pairs = jnp.stack([grad_key_rows, grad_value_rows], axis=1)
    window_grad = jnp.zeros((2, 2 * tok_count, HEAD_DIM), jnp.float32)
    begin = tok_count - (band_len - 1) * BLOCK
    window_grad = window_grad.at[:, begin : begin + band_len * BLOCK].add(
        grad_pairs[0, :, : band_len * BLOCK]
    )
    returned = from_behind(
        window_grad[:, :tok_count].astype(jnp.bfloat16), ("blk", "inner"), -1
    ).astype(jnp.float32)
    own_grad = window_grad[:, tok_count:] + returned
    stripe_grads = grad_pairs[:, :, band_len * BLOCK :].reshape(
        blocks_dev, 2, stripes, BLOCK * HEAD_DIM
    )
    stripe_grads = jnp.transpose(stripe_grads, (0, 2, 1, 3)).reshape(
        blocks_dev * stripes, 2, BLOCK * HEAD_DIM
    )
    selector = (
        anchor_ids.reshape(-1)[:, None] == jnp.arange(groups, dtype=jnp.int32)[None, :]
    ).astype(jnp.float32)
    anchor_grad = jnp.einsum("en,exy->nxy", selector, stripe_grads, precision=lax.Precision.HIGHEST)
    anchor_grad = anchor_grad.reshape(groups, 2, BLOCK, HEAD_DIM)
    column_grad = lax.psum_scatter(
        anchor_grad.astype(jnp.bfloat16), "blk", scatter_dimension=0, tiled=True
    ).astype(jnp.float32)
    group_grad = lax.psum(column_grad[0], "inner")
    is_root = lax.axis_index("inner") == 0
    own_grad = own_grad.at[:, :BLOCK].add(jnp.where(is_root, group_grad, 0.0))
    return (
        attended.reshape(tok_count, HEADS * HEAD_DIM),
        grad_queries.reshape(tok_count, HEADS * HEAD_DIM),
        own_grad[0],
        own_grad[1],
    )


def solution(mesh):
    in_specs = (
        P(("blk", "inner"), None),
        P(("blk", "inner"), None),
        P(("blk", "inner"), None),
        P(("blk", "inner"), None),
        P(("blk", "inner"), None),
    )
    out_specs = (
        P(("blk", "inner"), None),
        P(("blk", "inner"), None),
        P(("blk", "inner"), None),
        P(("blk", "inner"), None),
    )
    return jax.shard_map(shards, mesh=mesh, in_specs=in_specs, out_specs=out_specs, check_vma=False)
```

profile of v0, /device:TPU:0, one launch (start us, length us, event | category | flops | bytes accessed | tf_op | source)
XLA Modules:
  0.0 206.3 jit_solution(18070775661744440685)
XLA Ops:
  7.2 0.8 pad_maximum_fusion.2
  8.0 4.9 %collective-permute-start = (bf16[2,128,128]{2,1,0:T(8,128)(2,1)S(1)}, bf16[2,128,128]{2,1,0:T(8,128)(2,1)S(1)}, u32[]{:S(2)}, u32[]{:S(2)}) collective-permute-start(bf16[2,128,128]{2,1,0:T(8,128)(2,1)S(1)} %pad_maximum_fusion.2), channel_id=1, source_target_pairs={{0,1},{1,2},{2,3},{3,4},{4,5},{5,6},{6,7},{7,8},{8,9},{9,10},{10,1... | collective-permute-start | bytes 196616 | tf_op jit(solution)/shard_map/ppermute | solution.py:17
  12.9 5.8 %all-gather = bf16[8,128,128]{2,1,0:T(8,128)(2,1)S(1)} all-gather(bf16[2,128,128]{2,1,0:T(8,128)(2,1)S(1)} %pad_maximum_fusion.2), channel_id=2, replica_groups=mesh['blk'=4,'inner'=8] {'blk'}, dimensions={0}, use_global_device_ids=true | all-gather | bytes 327680 | tf_op jit(solution)/shard_map/all_gather | solution.py:40
  18.7 0.7 broadcast_select_fusion
  19.5 0.7 fusion.40
  20.3 0.8 compare_reduce_fusion
  21.9 0.2 compare_and_fusion
  22.1 1.7 copy.72
  23.9 0.8 maximum_bitcast_fusion.1
  24.7 65.9 %all-reduce.3.cloned.1.call-done = bf16[4,2,128,128]{3,2,1,0:T(8,128)(2,1)} async-done(((bf16[4,2,128,128]{3,2,1,0:T(8,128)(2,1)}), bf16[4,2,128,128]{3,2,1,0:T(8,128)(2,1)}) %all-reduce.3.cloned.1.call-update) | async-done | bytes 262160 | tf_op jit(solution)/shard_map/psum | solution.py:22
  90.5 1.5 gather_fusion
  92.1 0.5 fusion.5
  92.6 0.5 fusion.4
  93.2 1.7 bitcast_convert_fusion
  94.9 1.5 fusion.15
  96.5 1.3 copy.63
  97.7 1.8 multiply_reduce_fusion
  99.5 0.9 copy.64
  100.4 2.1 %fusion.6 = bf16[8,128,640]{1,2,0:T(8,128)(2,1)S(1)} fusion(f32[8,128]{1,0:T(8,128)S(1)} %copy.64, f32[8,128]{1,0:T(8,128)S(1)} %fusion.4, f32[8,128]{1,0:T(8,128)S(1)} %get-tuple-element.66, f32[640,128,8]{1,0,2:T(8,128)S(1)} %get-tuple-element.67, pred[128,640]{0,1:T(8,128)(4,1)} %copy-done.6, bf16[1,2,256,128]{3,2,1,0:T(8,128)(2,1)S(1)} %maximum_bitcast_fusion.1, ...), kind=kOutput, calls=%fused_computation.10 | convolution fusion | flops 173342720 | bytes 4616192 | tf_op jit(solution)/shard_map/rgao,rmo->ragm/dot_general | solution.py:89
  102.5 1.1 copy-done.1
  103.6 0.5 convolution_bitcast_fusion
  104.3 0.6 fusion.18
  105.0 0.7 copy.90
  105.8 1.3 collective-permute-start.1
  107.1 18.1 %reduce-scatter.2.cloned.1.call-done = bf16[1,2,128,128]{3,2,1,0:T(8,128)(2,1)} async-done(((bf16[4,2,128,128]{3,2,1,0:T(8,128)(2,1)}), bf16[1,2,128,128]{3,2,1,0:T(8,128)(2,1)}) %reduce-scatter.2.cloned.1.call-update) | async-done | bytes 65552 | tf_op jit(solution)/shard_map/reduce_scatter | solution.py:126
  125.2 1.5 bitcast_convert_fusion.1
  126.7 0.4 convolution_convert_fusion
  127.2 0.9 copy.54
  128.0 0.8 copy.55
  128.9 69.3 %all-reduce.5.cloned.1.call-done = f32[2,128,128]{2,1,0:T(8,128)} async-done(((f32[2,128,128]{2,1,0:T(8,128)}), f32[2,128,128]{2,1,0:T(8,128)}) %all-reduce.5.cloned.1.call-update) | async-done | bytes 131088 | tf_op jit(solution)/shard_map/psum | solution.py:129
  198.2 0.9 fusion.32
  199.1 0.7 slice_bitcast_fusion
  (44 shorter events, 1.2 us)
Async XLA Ops:
  7.2 84.9 %copy-start = (bf16[128,1024]{1,0:T(8,128)(2,1)S(1)}, bf16[128,1024]{1,0:T(8,128)(2,1)}, u32[]{:S(2)}) copy-start(bf16[128,1024]{1,0:T(8,128)(2,1)} %param.13) | copy-start | bytes 786436
  7.2 83.3 %all-reduce.3.cloned.1.call-start = ((), (), s32[]{:S(2)}) async-start(), calls=%async_computation.1 | async-start | bytes 524288 | tf_op jit(solution)/shard_map/psum | solution.py:22
  8.0 15.8 %collective-permute-start = (bf16[2,128,128]{2,1,0:T(8,128)(2,1)S(1)}, bf16[2,128,128]{2,1,0:T(8,128)(2,1)S(1)}, u32[]{:S(2)}, u32[]{:S(2)}) collective-permute-start(bf16[2,128,128]{2,1,0:T(8,128)(2,1)S(1)} %pad_maximum_fusion.2), channel_id=1, source_target_pairs={{0,1},{1,2},{2,3},{3,4},{4,5},{5,6},{6,7},{7,8},{8,9},{9,10},{10,1... | collective-permute-start | bytes 196616 | tf_op jit(solution)/shard_map/ppermute | solution.py:17
  19.5 105.7 %reduce-scatter.2.cloned.1.call-start = ((), (), s32[]{:S(2)}) async-start(), calls=%async_computation.2 | async-start | bytes 327680 | tf_op jit(solution)/shard_map/reduce_scatter | solution.py:126
  22.1 72.8 %copy-start.6 = (pred[128,640]{0,1:T(8,128)(4,1)}, pred[128,640]{0,1:T(8,128)(4,1)S(1)}, u32[]{:S(2)}) copy-start(pred[128,640]{0,1:T(8,128)(4,1)S(1)} %compare_and_fusion) | copy-start | bytes 245764
  92.1 1.1 copy-start.3
  93.2 1.7 copy-start.7
  100.4 3.7 %copy-start.5 = (f32[1,1,640,128]{3,2,1,0:T(8,128)S(1)}, f32[1,1,640,128]{3,2,1,0:T(8,128)}, u32[]{:S(2)}) copy-start(f32[1,1,640,128]{3,2,1,0:T(8,128)} %fusion.15) | copy-start | bytes 983044
  102.5 1.1 copy-start.1
  104.1 22.6 %copy-start.2 = (bf16[8,128,640]{1,2,0:T(8,128)(2,1)S(1)}, bf16[8,128,640]{1,2,0:T(8,128)(2,1)}, u32[]{:S(2)}) copy-start(bf16[8,128,640]{1,2,0:T(8,128)(2,1)} %copy-done.1) | copy-start | bytes 3932164
  104.1 22.6 %copy-start.4 = (bf16[1,2,3,128,128]{4,3,2,1,0:T(8,128)(2,1)S(1)}, bf16[1,2,3,128,128]{4,3,2,1,0:T(8,128)(2,1)}, u32[]{:S(2)}) copy-start(bf16[1,2,3,128,128]{4,3,2,1,0:T(8,128)(2,1)} %copy-done.3) | copy-start | bytes 589828
  104.9 22.2 %copy-start.8 = (bf16[128,8,128]{2,0,1:T(8,128)(2,1)S(1)}, bf16[128,8,128]{2,0,1:T(8,128)(2,1)}, u32[]{:S(2)}) copy-start(bf16[128,8,128]{2,0,1:T(8,128)(2,1)} %get-tuple-element.69) | copy-start | bytes 786436
  105.7 92.5 %all-reduce.5.cloned.1.call-start = ((), (), s32[]{:S(2)}) async-start(), calls=%async_computation.3 | async-start | bytes 262144 | tf_op jit(solution)/shard_map/psum | solution.py:129
  105.8 23.0 %collective-permute-start.1 = (bf16[2,128,128]{2,1,0:T(8,128)(2,1)S(1)}, bf16[2,128,128]{2,1,0:T(8,128)(2,1)S(1)}, u32[]{:S(2)}, u32[]{:S(2)}) collective-permute-start(bf16[2,128,128]{2,1,0:T(8,128)(2,1)S(1)} %slice.106), channel_id=1, source_target_pairs={{1,0},{2,1},{3,2},{4,3},{5,4},{6,5},{7,6},{8,7},{9,8},{10,9},{11,1... | collective-permute-start | bytes 196616 | tf_op jit(solution)/shard_map/ppermute | solution.py:17
Sparse Core Ops, SparseCore 0:
  19.6 70.9 all-reduce.2
  105.8 19.2 reduce-scatter.1
  128.5 69.5 all-reduce.4
where the time goes:
time: 207 us; the launch traced here: 206 us
  waiting for transfers between devices  153 us (74%)
  between operations  14 us (7%)
  local copies, waits for them, and re-layouts  10 us (5%)
  other arithmetic  9.53 us (5%)
  matrix products  7.35 us (4%)
  starting transfers between devices  6.27 us (3%)
  blocking collectives  5.79 us (3%)
    psum x1, waiting for transfers between devices, shards(): group_grad = lax.psum(column_grad[0], 'inner')  69.3 us
    psum x1, waiting for transfers between devices, broadcast(): return lax.psum(jnp.where(mine, value, jnp.zeros_like(value)), axis)  65.9 us
    reduce_scatter x1, waiting for transfers between devices, shards(): lax.psum_scatter(anchor_grad.astype(jnp.bfloat16), 'blk', scatter_dimensi...  18.1 us
    ppermute x2, starting transfers between devices, from_behind(): return lax.ppermute(block, axis, route)  6.15 us
    unnamed x22, local copies, waits for them, and re-layouts  5.8 us
    all_gather x1, blocking collectives, shards(): column = lax.all_gather(pair[None], 'blk', axis=0, tiled=True)  5.79 us
  transfers between devices with their start and end apart: 5, of which 3 were waited for; matrix products, arithmetic and copies ran while one was open for 5% of the time, Pallas kernels for 0%

commit v1 on v0

--- a/solution.py
+++ b/solution.py
@@ -19,7 +19,7 @@
 
 def broadcast(value, axis, root):
     mine = lax.axis_index(axis) == root
-    return lax.psum(jnp.where(mine, value, jnp.zeros_like(value)), axis)
+    return jnp.sum(lax.all_gather(jnp.where(mine, value, jnp.zeros_like(value)), axis), axis=0)
 
 
 def shards(queries, keys, values, out_grad, block_list):

time: 207 us -> 184 us (0.89)
  waiting for transfers between devices: 153 us -> 129 us
    psum x1 -> x0, waiting for transfers between devices: 65.9 us -> none  [broadcast(): return lax.psum(jnp.where(mine, value, jnp.zeros_like(value)), axis)]
    all_gather x0 -> x1, waiting for transfers between devices: none -> 42.2 us  [broadcast(): lax.all_gather(jnp.where(mine, value, jnp.zeros_like(value)), axis)]
where the time goes in v1:
time: 184 us; the launch traced here: 183 us
  waiting for transfers between devices  129 us (70%)
  between operations  14 us (8%)
  other arithmetic  11.5 us (6%)
  local copies, waits for them, and re-layouts  9.01 us (5%)
  matrix products  7.36 us (4%)
  blocking collectives  7.18 us (4%)
  starting transfers between devices  4.88 us (3%)
    psum x1, waiting for transfers between devices, shards(): group_grad = lax.psum(column_grad[0], 'inner')  69.7 us
    all_gather x1, waiting for transfers between devices, broadcast(): lax.all_gather(jnp.where(mine, value, jnp.zeros_like(value)), axis)  42.2 us
    reduce_scatter x1, waiting for transfers between devices, shards(): lax.psum_scatter(anchor_grad.astype(jnp.bfloat16), 'blk', scatter_dimensi...  17.3 us
    all_gather x1, blocking collectives, shards(): column = lax.all_gather(pair[None], 'blk', axis=0, tiled=True)  7.18 us
    unnamed x22, local copies, waits for them, and re-layouts  5.77 us
    ppermute x2, starting transfers between devices, from_behind(): return lax.ppermute(block, axis, route)  4.76 us
  transfers between devices with their start and end apart: 5, of which 3 were waited for; matrix products, arithmetic and copies ran while one was open for 5% of the time, Pallas kernels for 0%

profile of v1, /device:TPU:0, one launch (start us, length us, event | category | flops | bytes accessed | tf_op | source)
XLA Modules:
  0.0 183.2 jit_solution(11919831789983466792)
XLA Ops:
  7.2 0.8 pad_maximum_fusion.2
  8.0 7.2 %all-gather = bf16[8,128,128]{2,1,0:T(8,128)(2,1)S(1)} all-gather(bf16[2,128,128]{2,1,0:T(8,128)(2,1)S(1)} %pad_maximum_fusion.2), channel_id=2, replica_groups=mesh['blk'=4,'inner'=8] {'blk'}, dimensions={0}, use_global_device_ids=true | all-gather | bytes 327680 | tf_op jit(solution)/shard_map/all_gather | solution.py:40
  15.2 0.7 broadcast_select_fusion
  16.0 3.5 %collective-permute-start = (bf16[2,128,128]{2,1,0:T(8,128)(2,1)S(1)}, bf16[2,128,128]{2,1,0:T(8,128)(2,1)S(1)}, u32[]{:S(2)}, u32[]{:S(2)}) collective-permute-start(bf16[2,128,128]{2,1,0:T(8,128)(2,1)S(1)} %pad_maximum_fusion.2), channel_id=1, source_target_pairs={{0,1},{1,2},{2,3},{3,4},{4,5},{5,6},{6,7},{7,8},{8,9},{9,10},{10,1... | collective-permute-start | bytes 196616 | tf_op jit(solution)/shard_map/ppermute | solution.py:17
  19.5 1.7 copy.72
  21.2 0.7 fusion.40
  22.2 0.8 compare_reduce_fusion
  23.8 0.8 maximum_bitcast_fusion.1
  24.6 42.2 %all-gather.4.cloned.1.call-done = bf16[32,2,128,128]{3,2,1,0:T(8,128)(2,1)} async-done(((bf16[4,2,128,128]{3,2,1,0:T(8,128)(2,1)}), bf16[32,2,128,128]{3,2,1,0:T(8,128)(2,1)}) %all-gather.4.cloned.1.call-update) | async-done | bytes 2097168 | tf_op jit(solution)/shard_map/all_gather | solution.py:22
  66.8 2.0 %reduce_sum.21 = bf16[4,2,128,128]{3,2,1,0:T(8,128)(2,1)S(1)} reduce(bf16[8,4,2,128,128]{4,3,2,1,0:T(8,128)(2,1)} %bitcast.175, bf16[]{:T(256)} %constant.105.clone.1), dimensions={0}, to_apply=%region_0.1 | reduce | flops 917504 | bytes 2359298 | tf_op jit(solution)/shard_map/reduce_sum | solution.py:22
  68.8 0.6 gather_fusion
  69.4 0.5 fusion.5
  70.0 0.5 fusion.4
  70.6 1.7 bitcast_convert_fusion
  72.3 1.5 fusion.15
  73.8 1.3 copy.63
  75.1 1.8 multiply_reduce_fusion
  76.9 0.9 copy.64
  77.8 2.1 %fusion.6 = bf16[8,128,640]{1,2,0:T(8,128)(2,1)S(1)} fusion(f32[8,128]{1,0:T(8,128)S(1)} %copy.64, f32[8,128]{1,0:T(8,128)S(1)} %fusion.4, f32[8,128]{1,0:T(8,128)S(1)} %get-tuple-element.66, f32[640,128,8]{1,0,2:T(8,128)S(1)} %get-tuple-element.67, pred[128,640]{0,1:T(8,128)(4,1)} %copy-done.6, bf16[1,2,256,128]{3,2,1,0:T(8,128)(2,1)S(1)} %maximum_bitcast_fusion.1, ...), kind=kOutput, calls=%fused_computation.10 | convolution fusion | flops 173342720 | bytes 4616192 | tf_op jit(solution)/shard_map/rgao,rmo->ragm/dot_general | solution.py:89
  79.9 1.1 copy-done.1
  80.9 0.5 convolution_bitcast_fusion
  81.7 0.6 fusion.18
  82.3 0.7 copy.90
  83.2 1.3 collective-permute-start.1
  84.5 17.3 %reduce-scatter.2.cloned.1.call-done = bf16[1,2,128,128]{3,2,1,0:T(8,128)(2,1)} async-done(((bf16[4,2,128,128]{3,2,1,0:T(8,128)(2,1)}), bf16[1,2,128,128]{3,2,1,0:T(8,128)(2,1)}) %reduce-scatter.2.cloned.1.call-update) | async-done | bytes 65552 | tf_op jit(solution)/shard_map/reduce_scatter | solution.py:126
  101.7 1.5 bitcast_convert_fusion.1
  103.3 0.4 convolution_convert_fusion
  103.7 0.9 copy.54
  104.5 0.8 copy.55
  105.4 69.7 %all-reduce.2.cloned.1.call-done = f32[2,128,128]{2,1,0:T(8,128)} async-done(((f32[2,128,128]{2,1,0:T(8,128)}), f32[2,128,128]{2,1,0:T(8,128)}) %all-reduce.2.cloned.1.call-update) | async-done | bytes 131088 | tf_op jit(solution)/shard_map/psum | solution.py:129
  175.1 0.9 fusion.32
  176.0 0.7 slice_bitcast_fusion
  (45 shorter events, 1.5 us)
Async XLA Ops:
  7.2 62.3 %copy-start = (bf16[128,1024]{1,0:T(8,128)(2,1)S(1)}, bf16[128,1024]{1,0:T(8,128)(2,1)}, u32[]{:S(2)}) copy-start(bf16[128,1024]{1,0:T(8,128)(2,1)} %param.13) | copy-start | bytes 786436
  7.2 59.7 %all-gather.4.cloned.1.call-start = ((), (), s32[]{:S(2)}) async-start(), calls=%async_computation.3 | async-start | bytes 2359296 | tf_op jit(solution)/shard_map/all_gather | solution.py:22
  16.0 85.8 %reduce-scatter.2.cloned.1.call-start = ((), (), s32[]{:S(2)}) async-start(), calls=%async_computation.1 | async-start | bytes 327680 | tf_op jit(solution)/shard_map/reduce_scatter | solution.py:126
  16.0 7.8 %collective-permute-start = (bf16[2,128,128]{2,1,0:T(8,128)(2,1)S(1)}, bf16[2,128,128]{2,1,0:T(8,128)(2,1)S(1)}, u32[]{:S(2)}, u32[]{:S(2)}) collective-permute-start(bf16[2,128,128]{2,1,0:T(8,128)(2,1)S(1)} %pad_maximum_fusion.2), channel_id=1, source_target_pairs={{0,1},{1,2},{2,3},{3,4},{4,5},{5,6},{6,7},{7,8},{8,9},{9,10},{10,1... | collective-permute-start | bytes 196616 | tf_op jit(solution)/shard_map/ppermute | solution.py:17
  23.8 48.5 %copy-start.6 = (pred[128,640]{0,1:T(8,128)(4,1)}, pred[128,640]{0,1:T(8,128)(4,1)S(1)}, u32[]{:S(2)}) copy-start(pred[128,640]{0,1:T(8,128)(4,1)S(1)} %compare_and_fusion) | copy-start | bytes 245764
  69.4 1.1 copy-start.3
  70.5 1.7 copy-start.7
  77.8 3.7 %copy-start.5 = (f32[1,1,640,128]{3,2,1,0:T(8,128)S(1)}, f32[1,1,640,128]{3,2,1,0:T(8,128)}, u32[]{:S(2)}) copy-start(f32[1,1,640,128]{3,2,1,0:T(8,128)} %fusion.15) | copy-start | bytes 983044
  79.9 1.1 copy-start.1
  81.4 21.8 %copy-start.2 = (bf16[8,128,640]{1,2,0:T(8,128)(2,1)S(1)}, bf16[8,128,640]{1,2,0:T(8,128)(2,1)}, u32[]{:S(2)}) copy-start(bf16[8,128,640]{1,2,0:T(8,128)(2,1)} %copy-done.1) | copy-start | bytes 3932164
  81.5 21.8 %copy-start.4 = (bf16[1,2,3,128,128]{4,3,2,1,0:T(8,128)(2,1)S(1)}, bf16[1,2,3,128,128]{4,3,2,1,0:T(8,128)(2,1)}, u32[]{:S(2)}) copy-start(bf16[1,2,3,128,128]{4,3,2,1,0:T(8,128)(2,1)} %copy-done.3) | copy-start | bytes 589828
  82.3 21.4 %copy-start.8 = (bf16[128,8,128]{2,0,1:T(8,128)(2,1)S(1)}, bf16[128,8,128]{2,0,1:T(8,128)(2,1)}, u32[]{:S(2)}) copy-start(bf16[128,8,128]{2,0,1:T(8,128)(2,1)} %get-tuple-element.69) | copy-start | bytes 786436
  83.1 92.0 %all-reduce.2.cloned.1.call-start = ((), (), s32[]{:S(2)}) async-start(), calls=%async_computation.2 | async-start | bytes 262144 | tf_op jit(solution)/shard_map/psum | solution.py:129
  83.2 22.2 %collective-permute-start.1 = (bf16[2,128,128]{2,1,0:T(8,128)(2,1)S(1)}, bf16[2,128,128]{2,1,0:T(8,128)(2,1)S(1)}, u32[]{:S(2)}, u32[]{:S(2)}) collective-permute-start(bf16[2,128,128]{2,1,0:T(8,128)(2,1)S(1)} %slice.106), channel_id=1, source_target_pairs={{1,0},{2,1},{3,2},{4,3},{5,4},{6,5},{7,6},{8,7},{9,8},{10,9},{11,1... | collective-permute-start | bytes 196616 | tf_op jit(solution)/shard_map/ppermute | solution.py:17
Sparse Core Ops, SparseCore 0:
  16.1 50.6 all-gather.3
  83.2 18.4 reduce-scatter.1
  105.4 69.6 all-reduce.1
